TPU v7x, 128 devices: a whole 4x4x4 slice. The times are simulated.
128 devices in a mesh: row: 8 (over z_lo, x), col: 16 (over y, z_hi, core).
Axes of the slice: x: 4, y: 4, z: 4 (z_hi: 2, z_lo: 2; z = z_hi * 2 + z_lo), core: 2. Of those that a mesh axis runs over, the one named last changes fastest.
Arguments:
- positions: float32 [3, 16384, 128], P(None, ('row', 'col')), may hold values from -6 to 6
- block_links: int32 [2, 16384], replicated, may hold values from 0 to 16383, as said below
- panel_points: int32 [8, 256], replicated, may hold values from 0 to 2097151
Outputs:
- smoothed: float32 [3, 32768, 128], P(None, ('row', 'col'))
- velocity: float32 [8, 3, 256], P('row', None, 'col')
Inputs may be any that keep to these rules, and one draw needn't show every extreme that they name: block_links[0, b] is an owner device, numbered in the order of row+col; block_links[1] is a permutation of the 16384 blocks whose cycles are the loops, and all blocks of one loop have one owner. The 128 blocks of one device, b // 128, include at most 2 of any one owner, and in every draw one owner has exactly 2 blocks on every device.
All inputs are finite; a program needn't handle non-finite values.
Results may differ from a plain program's by a relative error of at most 0.0003.
Values sent between devices are 32-bit elements; how exact they have to be, the bound alone decides.
A program may use at most 128 MiB of HBM per device.

v0:
```python
import math
import jax
import jax.numpy as jnp
from jax import lax
from jax.sharding import PartitionSpec as P

SWEEPS = 2
SMOOTH_RATE = 0.25
CORE_SQUARED = 0.01


def cross_three(left_vec, right_vec):
    return jnp.stack(
        [
            left_vec[1] * right_vec[2] - left_vec[2] * right_vec[1],
            left_vec[2] * right_vec[0] - left_vec[0] * right_vec[2],
            left_vec[0] * right_vec[1] - left_vec[1] * right_vec[0],
        ]
    )


def neighbours(points, next_slot, prev_slot):
    ahead = jnp.concatenate([points[:, :, 1:], points[:, next_slot, :1]], axis=2)
    behind = jnp.concatenate([points[:, prev_slot, -1:], points[:, :, :-1]], axis=2)
    return (behind, ahead)


def smooth_loops(points, next_slot, prev_slot):
    for sweep_no in range(SWEEPS):
        behind, ahead = neighbours(points, next_slot, prev_slot)
        points = points + SMOOTH_RATE * (behind - 2.0 * points + ahead)
    return points


def panel_sums(targets, sources):
    centres = sources[:3]
    segments = sources[3:]
    inner = lax.dot_general(
        targets, centres, (((0,), (0,)), ((), ())), precision=lax.Precision.HIGHEST
    )
    squared = (
        jnp.sum(targets * targets, 0)[:, None]
        + jnp.sum(centres * centres, 0)[None, :]
        - 2.0 * inner
        + CORE_SQUARED
    )
    weights = 1.0 / (squared * jnp.sqrt(squared))
    features = jnp.concatenate([segments, cross_three(segments, centres)], 0)
    return lax.dot_general(
        weights, features, (((1,), (1,)), ((), ())), precision=lax.Precision.HIGHEST
    )


def tiled_sums(targets, piece, running, largest):
    blocks = piece.shape[1]
    block_len = piece.shape[2]
    group = max(
        [
            size_try
            for size_try in (1, 2, 4, 8, 16, 32, 64, 128)
            if blocks % size_try == 0 and size_try <= largest
        ]
    )

    def one_tile(turn, accum):
        tile = lax.dynamic_slice_in_dim(piece, turn * group, group, 1).reshape(6, group * block_len)
        return accum + panel_sums(targets, tile)

    return lax.fori_loop(0, blocks // group, one_tile, running)


def shards(positions, block_links, panel_points):
    devices = lax.axis_size(("row", "col"))
    my_index = lax.axis_index(("row", "col"))
    slots = positions.shape[1]
    block_len = positions.shape[2]
    capacity = 2 * slots // devices
    held_slots = devices * capacity
    owners = block_links[0]
    follows = block_links[1]
    blocks_all = owners.shape[0]
    counter = jnp.arange(blocks_all, dtype=jnp.int32)
    precedes = jnp.zeros_like(follows).at[follows].set(counter)
    owner_grid = owners.reshape(devices, slots)
    same_owner = owner_grid[:, :, None] == owner_grid[:, None, :]
    earlier = jnp.arange(slots)[None, :] < jnp.arange(slots)[:, None]
    ranks = jnp.sum(jnp.logical_and(same_owner, earlier[None]), axis=2).reshape(blocks_all)
    places = counter // slots * capacity + ranks
    my_owner = lax.dynamic_slice_in_dim(owners, my_index * slots, slots)
    my_rank = lax.dynamic_slice_in_dim(ranks, my_index * slots, slots)
    outgoing_slot = my_owner * capacity + my_rank
    outgoing = (
        jnp.zeros((3, held_slots, block_len), jnp.float32).at[:, outgoing_slot, :].set(positions)
    )
    arrived = lax.all_to_all(outgoing, ("row", "col"), split_axis=1, concat_axis=1, tiled=True)
    is_owned = owners == my_index
    held_ids = (
        jnp.full((held_slots,), blocks_all, jnp.int32)
        .at[jnp.where(is_owned, places, held_slots)]
        .set(counter, mode="drop")
    )
    live = held_ids < blocks_all
    safe_ids = jnp.minimum(held_ids, blocks_all - 1)
    slot_index = jnp.arange(held_slots, dtype=jnp.int32)
    next_slot = jnp.where(live, places[follows[safe_ids]], slot_index)
    prev_slot = jnp.where(live, places[precedes[safe_ids]], slot_index)
    smoothed = smooth_loops(arrived, next_slot, prev_slot)
    behind, ahead = neighbours(smoothed, next_slot, prev_slot)
    segments = ahead - smoothed
    centres = 0.5 * (ahead + smoothed)
    sources = jnp.concatenate([centres, segments], 0)
    wanted = panel_points.reshape(-1)
    wanted_block = wanted // block_len
    wanted_point = wanted % block_len
    wanted_mine = owners[wanted_block] == my_index
    picked = smoothed[:, places[wanted_block], wanted_point]
    local_targets = jnp.where(wanted_mine[None, :], picked, 0.0)
    all_targets = lax.psum(local_targets, ("row", "col"))
    panel = panel_points.shape[1]
    col_count = lax.axis_size("col")
    share = panel // col_count
    scale = 1.0 / (math.pi * math.sqrt(blocks_all * block_len))
    targets = lax.dynamic_slice_in_dim(all_targets, lax.axis_index("row") * panel, panel, 1)
    zero_sums = jnp.zeros((panel, 6), jnp.float32)
    sums = tiled_sums(targets, lax.all_gather(sources, "row", axis=1, tiled=True), zero_sums, 128)
    partial_velocity = scale * (cross_three(sums[:, :3].T, targets) - sums[:, 3:].T)
    summed = lax.psum(partial_velocity, "col")
    velocity_part = lax.dynamic_slice_in_dim(summed, lax.axis_index("col") * share, share, 1)
    return (smoothed, velocity_part[None])


def solution(mesh):
    placed = (P(None, ("row", "col"), None), P(), P())
    return jax.shard_map(
        shards,
        mesh=mesh,
        in_specs=placed,
        out_specs=(P(None, ("row", "col"), None), P("row", None, "col")),
        check_vma=False,
    )
```

profile of v0, /device:TPU:0, one launch (start us, length us, event | category | flops | bytes accessed | tf_op | source)
XLA Modules:
  0.0 976.3 jit_solution(4487103491891929501)
XLA Ops:
  7.2 1.1 fusion.56
  9.4 5.1 convert_reduce_fusion
  15.4 12.5 %scatter_fusion = f32[3,256,128]{2,0,1:T(4,128)} fusion(f32[3,256,128]{2,0,1:T(4,128)} %broadcast_in_dim.36, s32[128]{0:T(128)S(1)} %compare_select_fusion.13, f32[128,3,128]{2,1,0:T(4,128)S(1)} %copy.77), kind=kCustom, calls=%fused_computation.12 | custom fusion | bytes 590336 | tf_op jit(solution)/shard_map/scatter | solution.py:93
  27.9 11.2 %all-to-all-start = ((f32[3,256,128]{2,0,1:T(4,128)}), f32[3,256,128]{2,0,1:T(4,128)S(1)}, u32[]{:S(2)}, u32[]{:S(2)}) async-start(f32[3,256,128]{2,0,1:T(4,128)} %scatter_fusion), calls=%async_computation | async-start | bytes 1048576 | tf_op jit(solution)/shard_map/all_to_all | solution.py:95
  39.2 1.2 compare_select_fusion.1
  40.4 60.3 %scatter_custom_fusion.1 = s32[256]{0:T(256)S(1)} fusion(s32[16384]{0:T(1024)S(1)} %bitcast.119, s32[16384]{0:T(1024)S(1)} %iota.31, s32[]{:T(128)} %constant.150.clone.1), kind=kCustom, calls=%fused_computation.120 | custom fusion | bytes 1028 | tf_op jit(solution)/shard_map/scatter | solution.py:100
  100.8 60.5 %scatter_custom_fusion.2 = s32[16384]{0:T(1024)S(1)} fusion(s32[16384]{0:T(1024)S(1)} %bitcast.118, s32[16384]{0:T(1024)S(1)} %iota.33, s32[]{:T(128)} %constant.144.clone.1), kind=kCustom, calls=%fused_computation.79 | custom fusion | bytes 65540 | tf_op jit(solution)/shard_map/scatter | solution.py:83
  161.3 1.7 gather_fusion.3
  163.0 1.7 gather_fusion
  164.8 1.7 gather_fusion.1
  166.5 1.7 gather_fusion.4
  168.3 8.3 copy.78
  176.6 2.3 gather_fusion.5
  178.9 2.3 gather_fusion.2
  181.2 1.7 copy.83
  182.9 1.7 copy.80
  186.0 8.3 copy.84
  194.3 2.3 gather_fusion.6
  196.6 2.3 gather_fusion.7
  199.0 1.7 copy.86
  200.6 1.7 copy.89
  203.4 8.7 copy.90
  212.1 2.3 gather_fusion.11
  214.4 1.7 copy.93
  217.9 11.8 %gather_fusion.9 = s32[2048]{0:T(1024)S(1)} fusion(s32[16384]{0:T(1024)S(1)} %fusion.28, s32[2048]{0:T(1024)S(1)} %broadcast_clamp_fusion), kind=kCustom, calls=%fused_computation.9 | custom fusion | bytes 24576 | tf_op jit(solution)/shard_map/gather | solution.py:116
  229.7 11.8 %gather_fusion.8 = s32[2048]{0:T(1024)S(1)} fusion(s32[16384]{0:T(1024)S(1)} %bitcast.99, s32[2048]{0:T(1024)S(1)} %broadcast_clamp_fusion), kind=kCustom, calls=%fused_computation.8 | custom fusion | bytes 24576 | tf_op jit(solution)/shard_map/gather | solution.py:115
  242.3 20.8 %gather_fusion.10 = f32[2048,3]{1,0:T(8,128)S(1)} fusion(f32[3,256,128]{0,2,1:T(8,128)} %copy.90, s32[2048]{0:T(1024)S(1)} %bitcast.100), kind=kCustom, calls=%fused_computation.10 | custom fusion | bytes 65536 | tf_op jit(solution)/shard_map/gather | solution.py:116
  263.5 80.3 %psum.14 = f32[3,2048]{0,1:T(8,128)S(1)} all-reduce(f32[3,2048]{0,1:T(8,128)S(1)} %select_bitcast_fusion), channel_id=1, replica_groups=mesh['row'=8,'col'=16] {'row','col'}, use_global_device_ids=true, to_apply=%region_4.5 | all-reduce | flops 6144 | bytes 49152 | tf_op jit(solution)/shard_map/psum | solution.py:118
  344.3 586.7 %while.16 = (s32[]{:T(128)}, f32[256,6]{0,1:T(8,128)S(1)}, f32[256]{0:T(256)S(1)}, f32[6,2048,128]{2,1,0:T(8,128)}, f32[3,256]{1,0:T(4,128)S(1)}, /*index=5*/s32...) while((s32[]{:T(128)}, f32[256,6]{0,1:T(8,128)S(1)}, ...), condition=%wide.region_8.9_spmd.clone, body=%wide.region_6.8_spmd.clone.sunk | while | flops 478678016 | bytes 36061472 | solution.py:69
  345.6 1.1 dynamic-slice_bitcast_fusion.4
  346.8 25.7 %sqrt_multiply_fusion.2 = f32[256,16384]{0,1:T(8,128)S(1)} fusion(f32[3,256]{1,0:T(4,128)S(1)} %get-tuple-element.277, f32[16384]{0:T(1024)S(1)} %bitcast.107, f32[256]{0:T(256)S(1)} %get-tuple-element.275, f32[1,3,128,128]{3,2,1,0:T(8,128)S(1)} %get-tuple-element.240), kind=kOutput, calls=%fused_computation.15.clone.1 | convolution fusion | flops 171966464 | bytes 17043456 | tf_op jit(solution)/shard_map/while/body/eval_jaxpr/dot_general | solution.py:38
  372.4 8.8 fusion.67
  383.4 25.7 %sqrt_multiply_fusion.2 = f32[256,16384]{0,1:T(8,128)S(1)} fusion(f32[3,256]{1,0:T(4,128)S(1)} %get-tuple-element.277, f32[16384]{0:T(1024)S(1)} %bitcast.107, f32[256]{0:T(256)S(1)} %get-tuple-element.275, f32[1,3,128,128]{3,2,1,0:T(8,128)S(1)} %get-tuple-element.240), kind=kOutput, calls=%fused_computation.15.clone.1 | convolution fusion | flops 171966464 | bytes 17043456 | tf_op jit(solution)/shard_map/while/body/eval_jaxpr/dot_general | solution.py:38
  409.1 8.8 fusion.67
  420.1 25.7 %sqrt_multiply_fusion.2 = f32[256,16384]{0,1:T(8,128)S(1)} fusion(f32[3,256]{1,0:T(4,128)S(1)} %get-tuple-element.277, f32[16384]{0:T(1024)S(1)} %bitcast.107, f32[256]{0:T(256)S(1)} %get-tuple-element.275, f32[1,3,128,128]{3,2,1,0:T(8,128)S(1)} %get-tuple-element.240), kind=kOutput, calls=%fused_computation.15.clone.1 | convolution fusion | flops 171966464 | bytes 17043456 | tf_op jit(solution)/shard_map/while/body/eval_jaxpr/dot_general | solution.py:38
  445.8 8.8 fusion.67
  456.8 25.7 %sqrt_multiply_fusion.2 = f32[256,16384]{0,1:T(8,128)S(1)} fusion(f32[3,256]{1,0:T(4,128)S(1)} %get-tuple-element.277, f32[16384]{0:T(1024)S(1)} %bitcast.107, f32[256]{0:T(256)S(1)} %get-tuple-element.275, f32[1,3,128,128]{3,2,1,0:T(8,128)S(1)} %get-tuple-element.240), kind=kOutput, calls=%fused_computation.15.clone.1 | convolution fusion | flops 171966464 | bytes 17043456 | tf_op jit(solution)/shard_map/while/body/eval_jaxpr/dot_general | solution.py:38
  482.4 8.8 fusion.67
  492.2 1.1 dynamic-slice_bitcast_fusion.4
  493.4 25.7 %sqrt_multiply_fusion.2 = f32[256,16384]{0,1:T(8,128)S(1)} fusion(f32[3,256]{1,0:T(4,128)S(1)} %get-tuple-element.277, f32[16384]{0:T(1024)S(1)} %bitcast.107, f32[256]{0:T(256)S(1)} %get-tuple-element.275, f32[1,3,128,128]{3,2,1,0:T(8,128)S(1)} %get-tuple-element.240), kind=kOutput, calls=%fused_computation.15.clone.1 | convolution fusion | flops 171966464 | bytes 17043456 | tf_op jit(solution)/shard_map/while/body/eval_jaxpr/dot_general | solution.py:38
  519.1 8.8 fusion.67
  530.1 25.7 %sqrt_multiply_fusion.2 = f32[256,16384]{0,1:T(8,128)S(1)} fusion(f32[3,256]{1,0:T(4,128)S(1)} %get-tuple-element.277, f32[16384]{0:T(1024)S(1)} %bitcast.107, f32[256]{0:T(256)S(1)} %get-tuple-element.275, f32[1,3,128,128]{3,2,1,0:T(8,128)S(1)} %get-tuple-element.240), kind=kOutput, calls=%fused_computation.15.clone.1 | convolution fusion | flops 171966464 | bytes 17043456 | tf_op jit(solution)/shard_map/while/body/eval_jaxpr/dot_general | solution.py:38
  555.7 8.8 fusion.67
  566.7 25.7 %sqrt_multiply_fusion.2 = f32[256,16384]{0,1:T(8,128)S(1)} fusion(f32[3,256]{1,0:T(4,128)S(1)} %get-tuple-element.277, f32[16384]{0:T(1024)S(1)} %bitcast.107, f32[256]{0:T(256)S(1)} %get-tuple-element.275, f32[1,3,128,128]{3,2,1,0:T(8,128)S(1)} %get-tuple-element.240), kind=kOutput, calls=%fused_computation.15.clone.1 | convolution fusion | flops 171966464 | bytes 17043456 | tf_op jit(solution)/shard_map/while/body/eval_jaxpr/dot_general | solution.py:38
  592.4 8.8 fusion.67
  603.4 25.7 %sqrt_multiply_fusion.2 = f32[256,16384]{0,1:T(8,128)S(1)} fusion(f32[3,256]{1,0:T(4,128)S(1)} %get-tuple-element.277, f32[16384]{0:T(1024)S(1)} %bitcast.107, f32[256]{0:T(256)S(1)} %get-tuple-element.275, f32[1,3,128,128]{3,2,1,0:T(8,128)S(1)} %get-tuple-element.240), kind=kOutput, calls=%fused_computation.15.clone.1 | convolution fusion | flops 171966464 | bytes 17043456 | tf_op jit(solution)/shard_map/while/body/eval_jaxpr/dot_general | solution.py:38
  629.0 8.8 fusion.67
  640.0 25.7 %sqrt_multiply_fusion.2 = f32[256,16384]{0,1:T(8,128)S(1)} fusion(f32[3,256]{1,0:T(4,128)S(1)} %get-tuple-element.277, f32[16384]{0:T(1024)S(1)} %bitcast.107, f32[256]{0:T(256)S(1)} %get-tuple-element.275, f32[1,3,128,128]{3,2,1,0:T(8,128)S(1)} %get-tuple-element.240), kind=kOutput, calls=%fused_computation.15.clone.1 | convolution fusion | flops 171966464 | bytes 17043456 | tf_op jit(solution)/shard_map/while/body/eval_jaxpr/dot_general | solution.py:38
  665.7 8.8 fusion.67
  676.7 25.7 %sqrt_multiply_fusion.2 = f32[256,16384]{0,1:T(8,128)S(1)} fusion(f32[3,256]{1,0:T(4,128)S(1)} %get-tuple-element.277, f32[16384]{0:T(1024)S(1)} %bitcast.107, f32[256]{0:T(256)S(1)} %get-tuple-element.275, f32[1,3,128,128]{3,2,1,0:T(8,128)S(1)} %get-tuple-element.240), kind=kOutput, calls=%fused_computation.15.clone.1 | convolution fusion | flops 171966464 | bytes 17043456 | tf_op jit(solution)/shard_map/while/body/eval_jaxpr/dot_general | solution.py:38
  702.4 8.8 fusion.67
  713.4 25.7 %sqrt_multiply_fusion.2 = f32[256,16384]{0,1:T(8,128)S(1)} fusion(f32[3,256]{1,0:T(4,128)S(1)} %get-tuple-element.277, f32[16384]{0:T(1024)S(1)} %bitcast.107, f32[256]{0:T(256)S(1)} %get-tuple-element.275, f32[1,3,128,128]{3,2,1,0:T(8,128)S(1)} %get-tuple-element.240), kind=kOutput, calls=%fused_computation.15.clone.1 | convolution fusion | flops 171966464 | bytes 17043456 | tf_op jit(solution)/shard_map/while/body/eval_jaxpr/dot_general | solution.py:38
  739.0 8.8 fusion.67
  750.0 25.7 %sqrt_multiply_fusion.2 = f32[256,16384]{0,1:T(8,128)S(1)} fusion(f32[3,256]{1,0:T(4,128)S(1)} %get-tuple-element.277, f32[16384]{0:T(1024)S(1)} %bitcast.107, f32[256]{0:T(256)S(1)} %get-tuple-element.275, f32[1,3,128,128]{3,2,1,0:T(8,128)S(1)} %get-tuple-element.240), kind=kOutput, calls=%fused_computation.15.clone.1 | convolution fusion | flops 171966464 | bytes 17043456 | tf_op jit(solution)/shard_map/while/body/eval_jaxpr/dot_general | solution.py:38
  775.7 8.8 fusion.67
  786.7 25.7 %sqrt_multiply_fusion.2 = f32[256,16384]{0,1:T(8,128)S(1)} fusion(f32[3,256]{1,0:T(4,128)S(1)} %get-tuple-element.277, f32[16384]{0:T(1024)S(1)} %bitcast.107, f32[256]{0:T(256)S(1)} %get-tuple-element.275, f32[1,3,128,128]{3,2,1,0:T(8,128)S(1)} %get-tuple-element.240), kind=kOutput, calls=%fused_computation.15.clone.1 | convolution fusion | flops 171966464 | bytes 17043456 | tf_op jit(solution)/shard_map/while/body/eval_jaxpr/dot_general | solution.py:38
  812.3 8.8 fusion.67
  823.3 25.7 %sqrt_multiply_fusion.2 = f32[256,16384]{0,1:T(8,128)S(1)} fusion(f32[3,256]{1,0:T(4,128)S(1)} %get-tuple-element.277, f32[16384]{0:T(1024)S(1)} %bitcast.107, f32[256]{0:T(256)S(1)} %get-tuple-element.275, f32[1,3,128,128]{3,2,1,0:T(8,128)S(1)} %get-tuple-element.240), kind=kOutput, calls=%fused_computation.15.clone.1 | convolution fusion | flops 171966464 | bytes 17043456 | tf_op jit(solution)/shard_map/while/body/eval_jaxpr/dot_general | solution.py:38
  849.0 8.8 fusion.67
  860.0 25.7 %sqrt_multiply_fusion.2 = f32[256,16384]{0,1:T(8,128)S(1)} fusion(f32[3,256]{1,0:T(4,128)S(1)} %get-tuple-element.277, f32[16384]{0:T(1024)S(1)} %bitcast.107, f32[256]{0:T(256)S(1)} %get-tuple-element.275, f32[1,3,128,128]{3,2,1,0:T(8,128)S(1)} %get-tuple-element.240), kind=kOutput, calls=%fused_computation.15.clone.1 | convolution fusion | flops 171966464 | bytes 17043456 | tf_op jit(solution)/shard_map/while/body/eval_jaxpr/dot_general | solution.py:38
  885.7 8.8 fusion.67
  896.7 25.7 %sqrt_multiply_fusion.2 = f32[256,16384]{0,1:T(8,128)S(1)} fusion(f32[3,256]{1,0:T(4,128)S(1)} %get-tuple-element.277, f32[16384]{0:T(1024)S(1)} %bitcast.107, f32[256]{0:T(256)S(1)} %get-tuple-element.275, f32[1,3,128,128]{3,2,1,0:T(8,128)S(1)} %get-tuple-element.240), kind=kOutput, calls=%fused_computation.15.clone.1 | convolution fusion | flops 171966464 | bytes 17043456 | tf_op jit(solution)/shard_map/while/body/eval_jaxpr/dot_general | solution.py:38
  922.3 8.8 fusion.67
  931.7 37.0 %psum.15 = f32[3,256]{1,0:T(4,128)S(1)} all-reduce(f32[3,256]{1,0:T(4,128)S(1)} %fusion.41), channel_id=1, replica_groups=mesh['row'=8,'col'=16] {'col'}, use_global_device_ids=true, to_apply=%region_9.10 | all-reduce | flops 768 | bytes 6144 | tf_op jit(solution)/shard_map/psum | solution.py:127
  (97 shorter events, 43.0 us)
Async XLA Ops:
  27.9 140.4 %all-to-all-start = ((f32[3,256,128]{2,0,1:T(4,128)}), f32[3,256,128]{2,0,1:T(4,128)S(1)}, u32[]{:S(2)}, u32[]{:S(2)}) async-start(f32[3,256,128]{2,0,1:T(4,128)} %scatter_fusion), calls=%async_computation | async-start | bytes 1048576 | tf_op jit(solution)/shard_map/all_to_all | solution.py:95
  39.1 305.2 %all-gather.2.cloned.1.call-start = ((), (), s32[]{:S(2)}) async-start(), calls=%async_computation.1 | async-start | bytes 7077888 | tf_op jit(solution)/shard_map/all_gather | solution.py:125
  194.3 23.4 %copy-start = (s32[8,256]{1,0:T(8,128)S(1)}, s32[8,256]{1,0:T(8,128)}, u32[]{:S(2)}) copy-start(s32[8,256]{1,0:T(8,128)} %param.7) | copy-start | bytes 24580
Sparse Core Ops, SparseCore 0:
  217.9 75.4 all-gather.1
where the time goes:
time: 982 us; the launch traced here: 976 us
  matrix products  550 us (56%)
  local copies, waits for them, and re-layouts  239 us (24%)
  blocking collectives  117 us (12%)
  other arithmetic  42.8 us (4%)
  between operations  14.6 us (1%)
  starting transfers between devices  11.2 us (1%)
    dot_general x16, matrix products, panel_sums(): lax.dot_general(targets, centres, (((0,), (0,)), ((), ())), precision=lax...  410 us
    dot_general x16, matrix products, panel_sums(): lax.dot_general(weights, features, (((1,), (1,)), ((), ())), precision=la...  140 us
    psum x1, blocking collectives, shards(): all_targets = lax.psum(local_targets, ('row', 'col'))  80.3 us
    scatter x1, local copies, waits for them, and re-layouts, shards(): precedes = jnp.zeros_like(follows).at[follows].set(counter)  60.5 us
    scatter x1, local copies, waits for them, and re-layouts, shards(): held_ids = jnp.full((held_slots,), blocks_all, jnp.int32).at[jnp.where(is...  60.3 us
    psum x1, blocking collectives, shards(): summed = lax.psum(partial_velocity, 'col')  37 us
    gather x2, local copies, waits for them, and re-layouts, shards(): picked = smoothed[:, places[wanted_block], wanted_point]  32.6 us
  transfers between devices with their start and end apart: 2, of which 0 were waited for; matrix products, arithmetic and copies ran while one was open for 18% of the time, Pallas kernels for 0%

commit v1 on v0

--- a/solution.py
+++ b/solution.py
@@ -3,6 +3,7 @@
 import jax.numpy as jnp
 from jax import lax
 from jax.sharding import PartitionSpec as P
+from jax.lax import all_gather
 
 SWEEPS = 2
 SMOOTH_RATE = 0.25
@@ -115,7 +116,8 @@
     wanted_mine = owners[wanted_block] == my_index
     picked = smoothed[:, places[wanted_block], wanted_point]
     local_targets = jnp.where(wanted_mine[None, :], picked, 0.0)
-    all_targets = lax.psum(local_targets, ("row", "col"))
+    pages_meet = lambda ax_name, original: jnp.sum(all_gather(original, axis_name=ax_name), axis=0)
+    all_targets = pages_meet(("row", "col"), local_targets)
     panel = panel_points.shape[1]
     col_count = lax.axis_size("col")
     share = panel // col_count

time: 982 us -> 1170 us (1.19)
  waiting for transfers between devices: 0.02 us -> 261 us
  blocking collectives: 117 us -> 37.6 us
    all_gather x0 -> x1, waiting for transfers between devices: none -> 192 us  [shards(): all_gather(original, axis_name=ax_name)]
    psum x1 -> x0, blocking collectives: 80.3 us -> none  [shards(): all_targets = lax.psum(local_targets, ('row', 'col'))]
    all_gather x1, waiting for transfers between devices: 0.01 us -> 68.8 us  [shards(): lax.all_gather(sources, 'row', axis=1, tiled=True)]
  transfers between devices with their start and end apart: 2 -> 3, of which waited for: 0 -> 2; matrix products, arithmetic and copies ran while one was open for 18% -> 14% of each run, Pallas kernels for 0% -> 0%
where the time goes in v1:
time: 1170 us; the launch traced here: 1160 us
  matrix products  550 us (47%)
  waiting for transfers between devices  261 us (22%)
  local copies, waits for them, and re-layouts  241 us (21%)
  other arithmetic  44.6 us (4%)
  blocking collectives  37.6 us (3%)
  between operations  14.6 us (1%)
    dot_general x16, matrix products, panel_sums(): lax.dot_general(targets, centres, (((0,), (0,)), ((), ())), precision=lax...  410 us
    all_gather x1, waiting for transfers between devices, shards(): all_gather(original, axis_name=ax_name)  192 us
    dot_general x16, matrix products, panel_sums(): lax.dot_general(weights, features, (((1,), (1,)), ((), ())), precision=la...  140 us
    all_gather x1, waiting for transfers between devices, shards(): lax.all_gather(sources, 'row', axis=1, tiled=True)  68.8 us
    scatter x1, local copies, waits for them, and re-layouts, shards(): precedes = jnp.zeros_like(follows).at[follows].set(counter)  60.5 us
    scatter x1, local copies, waits for them, and re-layouts, shards(): held_ids = jnp.full((held_slots,), blocks_all, jnp.int32).at[jnp.where(is...  60.3 us
    psum x1, blocking collectives, shards(): summed = lax.psum(partial_velocity, 'col')  37.6 us
    gather x2, local copies, waits for them, and re-layouts, shards(): picked = smoothed[:, places[wanted_block], wanted_point]  32.8 us
  transfers between devices with their start and end apart: 3, of which 2 were waited for; matrix products, arithmetic and copies ran while one was open for 14% of the time, Pallas kernels for 0%

profile of v1, /device:TPU:0, one launch (start us, length us, event | category | flops | bytes accessed | tf_op | source)
XLA Modules:
  0.0 1161.3 jit_solution(13970231967604449137)
XLA Ops:
  7.2 1.1 fusion.56
  9.4 5.1 convert_reduce_fusion
  15.5 12.5 %scatter_fusion = f32[3,256,128]{2,0,1:T(4,128)} fusion(f32[3,256,128]{2,0,1:T(4,128)} %broadcast_in_dim.36, s32[128]{0:T(128)S(1)} %compare_select_fusion.13, f32[128,3,128]{2,1,0:T(4,128)S(1)} %copy.97), kind=kCustom, calls=%fused_computation.12 | custom fusion | bytes 590336 | tf_op jit(solution)/shard_map/scatter | solution.py:94
  28.0 11.1 all-to-all-start
  40.0 11.8 %gather_fusion.8 = s32[2048]{0:T(1024)S(1)} fusion(s32[16384]{0:T(1024)S(1)} %bitcast.101, s32[2048]{0:T(1024)S(1)} %broadcast_clamp_fusion), kind=kCustom, calls=%fused_computation.8 | custom fusion | bytes 24576 | tf_op jit(solution)/shard_map/gather | solution.py:116
  51.8 11.8 %gather_fusion.9 = s32[2048]{0:T(1024)S(1)} fusion(s32[16384]{0:T(1024)S(1)} %fusion.28, s32[2048]{0:T(1024)S(1)} %broadcast_clamp_fusion), kind=kCustom, calls=%fused_computation.9 | custom fusion | bytes 24576 | tf_op jit(solution)/shard_map/gather | solution.py:117
  63.8 60.3 %scatter_custom_fusion.1 = s32[256]{0:T(256)S(1)} fusion(s32[16384]{0:T(1024)S(1)} %bitcast.121, s32[16384]{0:T(1024)S(1)} %iota.31, s32[]{:T(128)} %constant.150.clone.1), kind=kCustom, calls=%fused_computation.119 | custom fusion | bytes 1028 | tf_op jit(solution)/shard_map/scatter | solution.py:101
  124.2 60.5 %scatter_custom_fusion.2 = s32[16384]{0:T(1024)S(1)} fusion(s32[16384]{0:T(1024)S(1)} %bitcast.120, s32[16384]{0:T(1024)S(1)} %iota.33, s32[]{:T(128)} %constant.144.clone.1), kind=kCustom, calls=%fused_computation.79 | custom fusion | bytes 65540 | tf_op jit(solution)/shard_map/scatter | solution.py:84
  184.7 1.7 gather_fusion.3
  186.4 1.7 gather_fusion
  188.2 1.7 gather_fusion.1
  189.9 1.7 gather_fusion.4
  191.8 8.3 copy.98
  200.0 2.3 gather_fusion.5
  202.4 2.3 gather_fusion.2
  204.7 1.7 copy.103
  206.4 1.7 copy.100
  209.5 8.3 copy.104
  217.8 2.3 gather_fusion.6
  220.1 2.3 gather_fusion.7
  222.5 1.7 copy.106
  224.1 1.7 copy.109
  226.5 8.3 copy.110
  234.8 21.0 %gather_fusion.10 = f32[2048,3]{1,0:T(8,128)S(1)} fusion(f32[3,256,128]{0,2,1:T(8,128)} %copy.110, s32[2048]{0:T(1024)S(1)} %bitcast.102), kind=kCustom, calls=%fused_computation.10 | custom fusion | bytes 65536 | tf_op jit(solution)/shard_map/gather | solution.py:117
  257.6 2.3 gather_fusion.11
  259.9 1.7 copy.115
  264.0 192.5 %all-gather.3.cloned.1.call-done = f32[128,3,2048]{2,1,0:T(4,128)} async-done(((f32[1,3,2048]{2,1,0:T(4,128)}), f32[128,3,2048]{2,1,0:T(4,128)}) %all-gather.3.cloned.1.call-update) | async-done | bytes 3145744 | tf_op jit(solution)/shard_map/all_gather | solution.py:119
  456.5 2.8 reduce_sum.45
  460.0 68.8 %all-gather.5.cloned.1.call-done = f32[6,2048,128]{2,1,0:T(8,128)} async-done(((f32[6,256,128]{2,1,0:T(8,128)}), f32[6,2048,128]{2,1,0:T(8,128)}) %all-gather.5.cloned.1.call-update) | async-done | bytes 6291472 | tf_op jit(solution)/shard_map/all_gather | solution.py:127
  528.7 586.7 %while.16 = (s32[]{:T(128)}, f32[256,6]{0,1:T(8,128)S(1)}, f32[256]{0:T(256)S(1)}, f32[6,2048,128]{2,1,0:T(8,128)}, f32[3,256]{1,0:T(4,128)S(1)}, /*index=5*/s32...) while((s32[]{:T(128)}, f32[256,6]{0,1:T(8,128)S(1)}, ...), condition=%wide.region_8.9_spmd.clone, body=%wide.region_6.8_spmd.clone.sunk | while | flops 478678016 | bytes 36061472 | solution.py:70
  531.2 25.7 %sqrt_multiply_fusion.2 = f32[256,16384]{0,1:T(8,128)S(1)} fusion(f32[3,256]{1,0:T(4,128)S(1)} %get-tuple-element.282, f32[16384]{0:T(1024)S(1)} %bitcast.109, f32[256]{0:T(256)S(1)} %get-tuple-element.280, f32[1,3,128,128]{3,2,1,0:T(8,128)S(1)} %get-tuple-element.245), kind=kOutput, calls=%fused_computation.15.clone.1 | convolution fusion | flops 171966464 | bytes 17043456 | tf_op jit(solution)/shard_map/while/body/eval_jaxpr/dot_general | solution.py:39
  556.8 8.8 fusion.67
  567.8 25.6 %sqrt_multiply_fusion.2 = f32[256,16384]{0,1:T(8,128)S(1)} fusion(f32[3,256]{1,0:T(4,128)S(1)} %get-tuple-element.282, f32[16384]{0:T(1024)S(1)} %bitcast.109, f32[256]{0:T(256)S(1)} %get-tuple-element.280, f32[1,3,128,128]{3,2,1,0:T(8,128)S(1)} %get-tuple-element.245), kind=kOutput, calls=%fused_computation.15.clone.1 | convolution fusion | flops 171966464 | bytes 17043456 | tf_op jit(solution)/shard_map/while/body/eval_jaxpr/dot_general | solution.py:39
  593.5 8.8 fusion.67
  604.5 25.7 %sqrt_multiply_fusion.2 = f32[256,16384]{0,1:T(8,128)S(1)} fusion(f32[3,256]{1,0:T(4,128)S(1)} %get-tuple-element.282, f32[16384]{0:T(1024)S(1)} %bitcast.109, f32[256]{0:T(256)S(1)} %get-tuple-element.280, f32[1,3,128,128]{3,2,1,0:T(8,128)S(1)} %get-tuple-element.245), kind=kOutput, calls=%fused_computation.15.clone.1 | convolution fusion | flops 171966464 | bytes 17043456 | tf_op jit(solution)/shard_map/while/body/eval_jaxpr/dot_general | solution.py:39
  630.1 8.8 fusion.67
  641.1 25.7 %sqrt_multiply_fusion.2 = f32[256,16384]{0,1:T(8,128)S(1)} fusion(f32[3,256]{1,0:T(4,128)S(1)} %get-tuple-element.282, f32[16384]{0:T(1024)S(1)} %bitcast.109, f32[256]{0:T(256)S(1)} %get-tuple-element.280, f32[1,3,128,128]{3,2,1,0:T(8,128)S(1)} %get-tuple-element.245), kind=kOutput, calls=%fused_computation.15.clone.1 | convolution fusion | flops 171966464 | bytes 17043456 | tf_op jit(solution)/shard_map/while/body/eval_jaxpr/dot_general | solution.py:39
  666.8 8.8 fusion.67
  677.8 25.7 %sqrt_multiply_fusion.2 = f32[256,16384]{0,1:T(8,128)S(1)} fusion(f32[3,256]{1,0:T(4,128)S(1)} %get-tuple-element.282, f32[16384]{0:T(1024)S(1)} %bitcast.109, f32[256]{0:T(256)S(1)} %get-tuple-element.280, f32[1,3,128,128]{3,2,1,0:T(8,128)S(1)} %get-tuple-element.245), kind=kOutput, calls=%fused_computation.15.clone.1 | convolution fusion | flops 171966464 | bytes 17043456 | tf_op jit(solution)/shard_map/while/body/eval_jaxpr/dot_general | solution.py:39
  703.5 8.8 fusion.67
  714.5 25.7 %sqrt_multiply_fusion.2 = f32[256,16384]{0,1:T(8,128)S(1)} fusion(f32[3,256]{1,0:T(4,128)S(1)} %get-tuple-element.282, f32[16384]{0:T(1024)S(1)} %bitcast.109, f32[256]{0:T(256)S(1)} %get-tuple-element.280, f32[1,3,128,128]{3,2,1,0:T(8,128)S(1)} %get-tuple-element.245), kind=kOutput, calls=%fused_computation.15.clone.1 | convolution fusion | flops 171966464 | bytes 17043456 | tf_op jit(solution)/shard_map/while/body/eval_jaxpr/dot_general | solution.py:39
  740.1 8.8 fusion.67
  749.9 1.1 dynamic-slice_bitcast_fusion.4
  751.1 25.7 %sqrt_multiply_fusion.2 = f32[256,16384]{0,1:T(8,128)S(1)} fusion(f32[3,256]{1,0:T(4,128)S(1)} %get-tuple-element.282, f32[16384]{0:T(1024)S(1)} %bitcast.109, f32[256]{0:T(256)S(1)} %get-tuple-element.280, f32[1,3,128,128]{3,2,1,0:T(8,128)S(1)} %get-tuple-element.245), kind=kOutput, calls=%fused_computation.15.clone.1 | convolution fusion | flops 171966464 | bytes 17043456 | tf_op jit(solution)/shard_map/while/body/eval_jaxpr/dot_general | solution.py:39
  776.8 8.8 fusion.67
  787.8 25.7 %sqrt_multiply_fusion.2 = f32[256,16384]{0,1:T(8,128)S(1)} fusion(f32[3,256]{1,0:T(4,128)S(1)} %get-tuple-element.282, f32[16384]{0:T(1024)S(1)} %bitcast.109, f32[256]{0:T(256)S(1)} %get-tuple-element.280, f32[1,3,128,128]{3,2,1,0:T(8,128)S(1)} %get-tuple-element.245), kind=kOutput, calls=%fused_computation.15.clone.1 | convolution fusion | flops 171966464 | bytes 17043456 | tf_op jit(solution)/shard_map/while/body/eval_jaxpr/dot_general | solution.py:39
  813.4 8.8 fusion.67
  824.4 25.7 %sqrt_multiply_fusion.2 = f32[256,16384]{0,1:T(8,128)S(1)} fusion(f32[3,256]{1,0:T(4,128)S(1)} %get-tuple-element.282, f32[16384]{0:T(1024)S(1)} %bitcast.109, f32[256]{0:T(256)S(1)} %get-tuple-element.280, f32[1,3,128,128]{3,2,1,0:T(8,128)S(1)} %get-tuple-element.245), kind=kOutput, calls=%fused_computation.15.clone.1 | convolution fusion | flops 171966464 | bytes 17043456 | tf_op jit(solution)/shard_map/while/body/eval_jaxpr/dot_general | solution.py:39
  850.1 8.8 fusion.67
  861.1 25.7 %sqrt_multiply_fusion.2 = f32[256,16384]{0,1:T(8,128)S(1)} fusion(f32[3,256]{1,0:T(4,128)S(1)} %get-tuple-element.282, f32[16384]{0:T(1024)S(1)} %bitcast.109, f32[256]{0:T(256)S(1)} %get-tuple-element.280, f32[1,3,128,128]{3,2,1,0:T(8,128)S(1)} %get-tuple-element.245), kind=kOutput, calls=%fused_computation.15.clone.1 | convolution fusion | flops 171966464 | bytes 17043456 | tf_op jit(solution)/shard_map/while/body/eval_jaxpr/dot_general | solution.py:39
  886.7 8.8 fusion.67
  897.7 25.7 %sqrt_multiply_fusion.2 = f32[256,16384]{0,1:T(8,128)S(1)} fusion(f32[3,256]{1,0:T(4,128)S(1)} %get-tuple-element.282, f32[16384]{0:T(1024)S(1)} %bitcast.109, f32[256]{0:T(256)S(1)} %get-tuple-element.280, f32[1,3,128,128]{3,2,1,0:T(8,128)S(1)} %get-tuple-element.245), kind=kOutput, calls=%fused_computation.15.clone.1 | convolution fusion | flops 171966464 | bytes 17043456 | tf_op jit(solution)/shard_map/while/body/eval_jaxpr/dot_general | solution.py:39
  923.4 8.8 fusion.67
  934.4 25.7 %sqrt_multiply_fusion.2 = f32[256,16384]{0,1:T(8,128)S(1)} fusion(f32[3,256]{1,0:T(4,128)S(1)} %get-tuple-element.282, f32[16384]{0:T(1024)S(1)} %bitcast.109, f32[256]{0:T(256)S(1)} %get-tuple-element.280, f32[1,3,128,128]{3,2,1,0:T(8,128)S(1)} %get-tuple-element.245), kind=kOutput, calls=%fused_computation.15.clone.1 | convolution fusion | flops 171966464 | bytes 17043456 | tf_op jit(solution)/shard_map/while/body/eval_jaxpr/dot_general | solution.py:39
  960.1 8.8 fusion.67
  971.1 25.7 %sqrt_multiply_fusion.2 = f32[256,16384]{0,1:T(8,128)S(1)} fusion(f32[3,256]{1,0:T(4,128)S(1)} %get-tuple-element.282, f32[16384]{0:T(1024)S(1)} %bitcast.109, f32[256]{0:T(256)S(1)} %get-tuple-element.280, f32[1,3,128,128]{3,2,1,0:T(8,128)S(1)} %get-tuple-element.245), kind=kOutput, calls=%fused_computation.15.clone.1 | convolution fusion | flops 171966464 | bytes 17043456 | tf_op jit(solution)/shard_map/while/body/eval_jaxpr/dot_general | solution.py:39
  996.7 8.8 fusion.67
  1007.7 25.7 %sqrt_multiply_fusion.2 = f32[256,16384]{0,1:T(8,128)S(1)} fusion(f32[3,256]{1,0:T(4,128)S(1)} %get-tuple-element.282, f32[16384]{0:T(1024)S(1)} %bitcast.109, f32[256]{0:T(256)S(1)} %get-tuple-element.280, f32[1,3,128,128]{3,2,1,0:T(8,128)S(1)} %get-tuple-element.245), kind=kOutput, calls=%fused_computation.15.clone.1 | convolution fusion | flops 171966464 | bytes 17043456 | tf_op jit(solution)/shard_map/while/body/eval_jaxpr/dot_general | solution.py:39
  1033.4 8.8 fusion.67
  1044.4 25.7 %sqrt_multiply_fusion.2 = f32[256,16384]{0,1:T(8,128)S(1)} fusion(f32[3,256]{1,0:T(4,128)S(1)} %get-tuple-element.282, f32[16384]{0:T(1024)S(1)} %bitcast.109, f32[256]{0:T(256)S(1)} %get-tuple-element.280, f32[1,3,128,128]{3,2,1,0:T(8,128)S(1)} %get-tuple-element.245), kind=kOutput, calls=%fused_computation.15.clone.1 | convolution fusion | flops 171966464 | bytes 17043456 | tf_op jit(solution)/shard_map/while/body/eval_jaxpr/dot_general | solution.py:39
  1070.0 8.8 fusion.67
  1081.0 25.7 %sqrt_multiply_fusion.2 = f32[256,16384]{0,1:T(8,128)S(1)} fusion(f32[3,256]{1,0:T(4,128)S(1)} %get-tuple-element.282, f32[16384]{0:T(1024)S(1)} %bitcast.109, f32[256]{0:T(256)S(1)} %get-tuple-element.280, f32[1,3,128,128]{3,2,1,0:T(8,128)S(1)} %get-tuple-element.245), kind=kOutput, calls=%fused_computation.15.clone.1 | convolution fusion | flops 171966464 | bytes 17043456 | tf_op jit(solution)/shard_map/while/body/eval_jaxpr/dot_general | solution.py:39
  1106.7 8.8 fusion.67
  1116.0 37.6 %psum.7 = f32[3,256]{1,0:T(4,128)S(1)} all-reduce(f32[3,256]{1,0:T(4,128)S(1)} %fusion.41), channel_id=1, replica_groups=mesh['row'=8,'col'=16] {'col'}, use_global_device_ids=true, to_apply=%region_9.10 | all-reduce | flops 768 | bytes 6144 | tf_op jit(solution)/shard_map/psum | solution.py:129
  (102 shorter events, 46.0 us)
Async XLA Ops:
  7.2 56.4 %copy-start = (s32[2,16384]{1,0:T(2,128)S(1)}, s32[2,16384]{1,0:T(2,128)}, u32[]{:S(2)}) copy-start(s32[2,16384]{1,0:T(2,128)} %param.6) | copy-start | bytes 393220
  28.0 163.8 %all-to-all-start = ((f32[3,256,128]{2,0,1:T(4,128)}), f32[3,256,128]{2,0,1:T(4,128)S(1)}, u32[]{:S(2)}, u32[]{:S(2)}) async-start(f32[3,256,128]{2,0,1:T(4,128)} %scatter_fusion), calls=%async_computation | async-start | bytes 1048576 | tf_op jit(solution)/shard_map/all_to_all | solution.py:96
  39.1 417.4 %all-gather.3.cloned.1.call-start = ((), (), s32[]{:S(2)}) async-start(), calls=%async_computation.1 | async-start | bytes 4227072 | tf_op jit(solution)/shard_map/all_gather | solution.py:119
  257.2 271.6 %all-gather.5.cloned.1.call-start = ((), (), s32[]{:S(2)}) async-start(), calls=%async_computation.2 | async-start | bytes 7077888 | tf_op jit(solution)/shard_map/all_gather | solution.py:127
Sparse Core Ops, SparseCore 0:
  257.3 199.1 all-gather.2
  458.1 70.5 all-gather.4
